TPU v7x, 512 devices: a whole 4x8x8 slice. The times are simulated.
512 devices in a mesh: region: 32 (over x, z), tm: 16 (over y, core).
Axes of the slice: x: 4, y: 8, z: 8, core: 2. Of those that a mesh axis runs over, the one named last changes fastest.
Arguments:
- right_side: float32 [1024, 65536], P('tm', 'region'), may hold values from -9 to 9
- initial: float32 [1024, 65536], P('tm', 'region'), may hold values from -1.5 to 1.5
- blocks: bfloat16 [512, 9, 128, 128], P(('region', 'tm')), may hold values from -2.5 to 3.1, as said below
- neighbour_blocks: int32 [512, 8], P('region'), may hold values from 0 to 511, as said below
- temporal_cov: bfloat16 [1024, 1024], P('tm'), may hold values from -2.5 to 2.8, as said below
Outputs:
- solution: float32 [1024, 65536], P('tm', 'region')
- residual: float32 [1024, 65536], P('tm', 'region')
Inputs may be any that keep to these rules, and one draw needn't show every extreme that they name: blocks[i, 0] is symmetric positive definite. `neighbour_blocks`: each column names every block exactly once. Blocks fall into cyclic windows of 16 consecutive blocks starting at 8 + m * 16, and every block listed for row i lies in the window of i. temporal_cov is symmetric positive definite.
All inputs are finite; a program needn't handle non-finite values.
Results may differ from a plain program's by a relative error of at most 0.012.
The roundings to bfloat16 on the way count: a program that leaves them out, or rounds other values in their place, can miss the bound.
Values may be sent and summed in bfloat16 or wider, within the bound.
No kernel may reach another device: no remote copies, remote signals or barrier semaphores. Data moves between devices by JAX's collectives and lax.ppermute only.
A program may use at most 64 MiB of HBM per device.

v0:
```python
import jax
import jax.numpy as jnp
from jax import lax
from jax.sharding import Mesh
from jax.sharding import PartitionSpec as P

ITERS = 2
REGION = ("region_0", "region_1")
TM = ("tm_0", "tm_1")
REGION_TM = ("region_0", "region_1", "tm_0", "tm_1")


def with_halo(value, sides, width):
    for axis, dim in sides:
        peers, length = (lax.axis_size(axis), value.shape[dim])
        up = [(i, (i + 1) % peers) for i in range(peers)]
        down = [(j, i) for i, j in up]
        last = lax.slice_in_dim(value, length - width, length, axis=dim)
        initial = lax.slice_in_dim(value, 0, width, axis=dim)
        before = lax.ppermute(last, axis, up)
        after = lax.ppermute(initial, axis, down)
        value = jnp.concatenate([before, value, after], axis=dim)
    return value


def gather_axes(value, axes, dim):
    for axis in reversed(axes):
        value = lax.all_gather(value, axis, axis=dim, tiled=True)
    return value


def one_axis_at_a_time(value, axes):
    for axis in axes:
        value = lax.psum(value, axis)
    return value


def local_tiles(lowered, neighbour_blocks):
    row_count = neighbour_blocks.shape[0]
    tile_width = lowered.shape[1] // row_count
    widened = with_halo(lowered, ((REGION, 1),), row_count // 2 * tile_width)
    region = lax.axis_index(REGION)
    block_total = row_count * lax.axis_size(REGION)
    offset = jnp.mod(neighbour_blocks - region * row_count + row_count // 2, block_total)
    itself = (jnp.arange(row_count, dtype=jnp.int32) + row_count // 2)[:, None]
    places = jnp.concatenate([itself, offset], axis=1)
    cell_tiles = widened.reshape(widened.shape[0], 2 * row_count, tile_width)
    return jnp.take(cell_tiles, places, axis=1)


def local(right_side, initial, blocks, neighbour_blocks, temporal_cov):
    hour_matrix = gather_axes(temporal_cov, TM, 0)
    region_blocks = lax.all_gather(blocks, TM, axis=0, tiled=True)
    tm_count = lax.axis_size(TM)
    hour_slice = right_side.shape[0]
    site_count = right_side.shape[1]
    tile_width = blocks.shape[2]
    own_rows = blocks.shape[0]

    def temporal(arrived):
        item_count = arrived.shape[2]
        flattened = arrived.reshape(arrived.shape[0], item_count * tile_width)
        blended = jnp.dot(hour_matrix, flattened, preferred_element_type=jnp.float32).astype(
            jnp.bfloat16
        )
        return blended.reshape(arrived.shape[0], 1, item_count, tile_width)

    def operate(current):
        lowered = current.astype(jnp.bfloat16)
        tile_stack = local_tiles(lowered, neighbour_blocks)
        spatial = jnp.einsum(
            "hrkb,rkab->hra", tile_stack, region_blocks, preferred_element_type=jnp.float32
        )
        spatial = spatial.astype(jnp.bfloat16).reshape(hour_slice, tm_count, own_rows, tile_width)
        blended = temporal(lax.all_to_all(spatial, TM, split_axis=1, concat_axis=0, tiled=True))
        returned = lax.all_to_all(blended, TM, split_axis=0, concat_axis=1, tiled=True)
        return current + returned.reshape(hour_slice, site_count).astype(jnp.float32)

    solution = initial
    residual = right_side - operate(initial)
    direction = residual
    norm_now = one_axis_at_a_time(jnp.sum(residual * residual), REGION_TM)
    for iteration in range(ITERS):
        applied = operate(direction)
        curvature, cross_term, square = (
            one_axis_at_a_time(jnp.sum(direction * applied), REGION_TM),
            one_axis_at_a_time(jnp.sum(residual * applied), REGION_TM),
            one_axis_at_a_time(jnp.sum(applied * applied), REGION_TM),
        )
        step_size = norm_now / curvature
        solution = solution + step_size * direction
        norm_next = norm_now - 2.0 * step_size * cross_term + step_size * step_size * square
        residual = residual - step_size * applied
        if iteration + 1 < ITERS:
            direction = residual + norm_next / norm_now * direction
        norm_now = norm_next
    return (solution, residual)


def solution(mesh):
    split = Mesh(mesh.devices.reshape(4, 8, 8, 2), ("region_0", "region_1", "tm_0", "tm_1"))
    return jax.shard_map(
        local,
        mesh=split,
        in_specs=(
            P(TM, REGION),
            P(TM, REGION),
            P(REGION_TM, None, None, None),
            P(REGION, None),
            P(TM, None),
        ),
        out_specs=(P(TM, REGION), P(TM, REGION)),
        check_vma=False,
    )
```

profile of v0, /device:TPU:1, one launch (start us, length us, event | category | flops | bytes accessed | tf_op | source)
XLA Modules:
  0.0 342.4 jit_solution(12038400127978279072)
XLA Ops:
  7.9 10.2 %all_gather.10 = bf16[128,1024]{1,0:T(8,128)(2,1)} all-gather(bf16[64,1024]{1,0:T(8,128)(2,1)} %param.11), channel_id=1, replica_groups=mesh['region_0'=4,'region_1'=8,'tm_0'=8,'tm_1'=2] {'tm_1'}, dimensions={0}, use_global_device_ids=true | all-gather | bytes 393216 | tf_op jit(solution)/shard_map/all_gather | solution.py:28
  21.2 7.5 %collective-permute-start.1 = (bf16[64,1024]{1,0:T(8,128)(2,1)S(1)}, bf16[64,1024]{1,0:T(8,128)(2,1)S(1)}, u32[]{:S(2)}, u32[]{:S(2)}) collective-permute-start(bf16[64,1024]{1,0:T(8,128)(2,1)S(1)} %get-tuple-element.27), channel_id=1, source_target_pairs={{16,0},{32,16},{48,32},{64,48},{80,64},{96,80},{112,96},{128,112},... | collective-permute-start | bytes 393224 | tf_op jit(solution)/shard_map/ppermute | solution.py:21
  32.6 27.8 %all-gather.3.cloned.1.call-done = bf16[16,9,128,128]{3,2,1,0:T(8,128)(2,1)} async-done(((bf16[1,9,128,128]{3,2,1,0:T(8,128)(2,1)}), bf16[16,9,128,128]{3,2,1,0:T(8,128)(2,1)}) %all-gather.3.cloned.1.call-update) | async-done | bytes 4718608 | tf_op jit(solution)/shard_map/all_gather | solution.py:53
  60.5 5.0 %fusion.36 = bf16[64,16,1,128]{3,0,2,1:T(8,128)(2,1)} fusion(bf16[16,9,128,128]{3,2,1,0:T(8,128)(2,1)} %all-gather.3.cloned.1.call-done, bf16[16,9,64,128]{3,2,1,0:T(8,128)(2,1)S(1)} %bitcast.174, pred[16,9]{1,0:T(8,128)(4,1)S(1)} %copy.40), kind=kOutput, calls=%fused_computation.30 | convolution fusion | flops 303300608 | bytes 7340176 | tf_op jit(solution)/shard_map/hrkb,rkab->hra/dot_general | solution.py:71
  65.5 5.0 %all-to-all-start = ((bf16[64,16,1,128]{3,0,2,1:T(8,128)(2,1)}), bf16[64,16,1,128]{3,0,2,1:T(8,128)(2,1)S(1)}, u32[]{:S(2)}, u32[]{:S(2)}) async-start(bf16[64,16,1,128]{3,0,2,1:T(8,128)(2,1)} %fusion.36), calls=%async_computation | async-start | bytes 524288 | tf_op jit(solution)/shard_map/all_to_all | solution.py:75
  70.5 31.9 %all-gather.5.cloned.1.call-done = bf16[1024,1024]{1,0:T(8,128)(2,1)} async-done(((bf16[128,1024]{1,0:T(8,128)(2,1)}), bf16[1024,1024]{1,0:T(8,128)(2,1)}) %all-gather.5.cloned.1.call-update) | async-done | bytes 2097168 | tf_op jit(solution)/shard_map/all_gather | solution.py:28
  106.3 20.0 %all_to_all.72 = bf16[16,2,4096]{2,1,0:T(2,128)(2,1)S(1)} all-to-all(bf16[16,2,4096]{2,1,0:T(2,128)(2,1)S(1)} %reshape.136), channel_id=1, replica_groups=mesh['region_0'=4,'region_1'=8,'tm_0'=8,'tm_1'=2] {'tm_0','tm_1'}, dimensions={0} | all-to-all | bytes 524288 | tf_op jit(solution)/shard_map/all_to_all | solution.py:76
  127.3 3.3 collective-permute-start.2
  130.6 6.4 %collective-permute-start.3 = (bf16[64,1024]{1,0:T(8,128)(2,1)S(1)}, bf16[64,1024]{1,0:T(8,128)(2,1)S(1)}, u32[]{:S(2)}, u32[]{:S(2)}) collective-permute-start(bf16[64,1024]{1,0:T(8,128)(2,1)S(1)} %get-tuple-element.25), channel_id=1, source_target_pairs={{16,0},{32,16},{48,32},{64,48},{80,64},{96,80},{112,96},{128,112},... | collective-permute-start | bytes 393224 | tf_op jit(solution)/shard_map/ppermute | solution.py:21
  142.7 5.1 %fusion.39 = bf16[64,16,1,128]{3,0,2,1:T(8,128)(2,1)S(1)} fusion(bf16[16,9,128,128]{3,2,1,0:T(8,128)(2,1)} %all-gather.3.cloned.1.call-done, bf16[16,9,64,128]{3,2,1,0:T(8,128)(2,1)} %bitcast.176, pred[16,9]{1,0:T(8,128)(4,1)S(1)} %copy.40), kind=kOutput, calls=%fused_computation.31 | convolution fusion | flops 303300608 | bytes 7340176 | tf_op jit(solution)/shard_map/hrkb,rkab->hra/dot_general | solution.py:71
  147.9 14.7 %all_to_all.73 = bf16[64,16,1,128]{3,0,2,1:T(8,128)(2,1)S(1)} all-to-all(bf16[64,16,1,128]{3,0,2,1:T(8,128)(2,1)S(1)} %fusion.39), channel_id=1, replica_groups=mesh['region_0'=4,'region_1'=8,'tm_0'=8,'tm_1'=2] {'tm_0','tm_1'}, dimensions={1} | all-to-all | bytes 524288 | tf_op jit(solution)/shard_map/all_to_all | solution.py:75
  164.5 14.2 %all_to_all.74 = bf16[16,2,4096]{2,1,0:T(2,128)(2,1)S(1)} all-to-all(bf16[16,2,4096]{2,1,0:T(2,128)(2,1)S(1)} %reshape.138), channel_id=1, replica_groups=mesh['region_0'=4,'region_1'=8,'tm_0'=8,'tm_1'=2] {'tm_0','tm_1'}, dimensions={0} | all-to-all | bytes 524288 | tf_op jit(solution)/shard_map/all_to_all | solution.py:76
  180.3 7.2 %all-reduce.2 = (f32[]{:T(128)}, f32[]{:T(128)}, f32[]{:T(128)}) all-reduce(f32[]{:T(128)} %get-tuple-element.5, f32[]{:T(128)} %get-tuple-element.4, f32[]{:T(128)} %get-tuple-element.3), channel_id=1, replica_groups=mesh['region_0'=4,'region_1'=8,'tm_0'=8,'tm_1'=2] {'region_0'}, use_global_device_ids=true, to_apply=%region_1.3 | all-reduce | flops 3 | bytes 24 | tf_op jit(solution)/shard_map/psum | solution.py:34
  187.5 16.8 %all-reduce.1 = (f32[]{:T(128)}, f32[]{:T(128)}, f32[]{:T(128)}) all-reduce(f32[]{:T(128)} %get-tuple-element.12, f32[]{:T(128)} %get-tuple-element.13, f32[]{:T(128)} %get-tuple-element.14), channel_id=1, replica_groups=mesh['region_0'=4,'region_1'=8,'tm_0'=8,'tm_1'=2] {'region_1'}, use_global_device_ids=true, to_apply=%region_2.4 | all-reduce | flops 3 | bytes 24 | tf_op jit(solution)/shard_map/psum | solution.py:34
  204.3 11.7 %all-reduce = (f32[]{:T(128)}, f32[]{:T(128)}, f32[]{:T(128)}) all-reduce(f32[]{:T(128)} %get-tuple-element.9, f32[]{:T(128)} %get-tuple-element.10, f32[]{:T(128)} %get-tuple-element.11), channel_id=1, replica_groups=mesh['region_0'=4,'region_1'=8,'tm_0'=8,'tm_1'=2] {'tm_0'}, use_global_device_ids=true, to_apply=%region_3.5 | all-reduce | flops 3 | bytes 24 | tf_op jit(solution)/shard_map/psum | solution.py:34
  216.0 11.5 %all-reduce.3 = (f32[]{:T(128)}, f32[]{:T(128)}, f32[]{:T(128)}) all-reduce(f32[]{:T(128)} %get-tuple-element.6, f32[]{:T(128)} %get-tuple-element.7, f32[]{:T(128)} %get-tuple-element.8), channel_id=1, replica_groups=mesh['region_0'=4,'region_1'=8,'tm_0'=8,'tm_1'=2] {'tm_1'}, use_global_device_ids=true, to_apply=%region_4.6 | all-reduce | flops 3 | bytes 24 | tf_op jit(solution)/shard_map/psum | solution.py:34
  233.3 6.7 %collective-permute-start.5 = (bf16[64,1024]{1,0:T(8,128)(2,1)S(1)}, bf16[64,1024]{1,0:T(8,128)(2,1)S(1)}, u32[]{:S(2)}, u32[]{:S(2)}) collective-permute-start(bf16[64,1024]{1,0:T(8,128)(2,1)S(1)} %get-tuple-element.23), channel_id=1, source_target_pairs={{16,0},{32,16},{48,32},{64,48},{80,64},{96,80},{112,96},{128,112},... | collective-permute-start | bytes 393224 | tf_op jit(solution)/shard_map/ppermute | solution.py:21
  244.9 5.0 %fusion.42 = bf16[64,16,1,128]{3,0,2,1:T(8,128)(2,1)S(1)} fusion(bf16[16,9,128,128]{3,2,1,0:T(8,128)(2,1)} %all-gather.3.cloned.1.call-done, bf16[16,9,64,128]{3,2,1,0:T(8,128)(2,1)} %bitcast.175, pred[16,9]{1,0:T(8,128)(4,1)S(1)} %copy.40), kind=kOutput, calls=%fused_computation.32 | convolution fusion | flops 303300608 | bytes 7340176 | tf_op jit(solution)/shard_map/hrkb,rkab->hra/dot_general | solution.py:71
  249.9 18.4 %all_to_all.75 = bf16[64,16,1,128]{3,0,2,1:T(8,128)(2,1)S(1)} all-to-all(bf16[64,16,1,128]{3,0,2,1:T(8,128)(2,1)S(1)} %fusion.42), channel_id=1, replica_groups=mesh['region_0'=4,'region_1'=8,'tm_0'=8,'tm_1'=2] {'tm_0','tm_1'}, dimensions={1} | all-to-all | bytes 524288 | tf_op jit(solution)/shard_map/all_to_all | solution.py:75
  270.1 14.5 %all_to_all.76 = bf16[16,2,4096]{2,1,0:T(2,128)(2,1)S(1)} all-to-all(bf16[16,2,4096]{2,1,0:T(2,128)(2,1)S(1)} %reshape.140), channel_id=1, replica_groups=mesh['region_0'=4,'region_1'=8,'tm_0'=8,'tm_1'=2] {'tm_0','tm_1'}, dimensions={0} | all-to-all | bytes 524288 | tf_op jit(solution)/shard_map/all_to_all | solution.py:76
  286.4 6.7 %psum.136 = f32[]{:T(128)} all-reduce(f32[]{:T(128)} %multiply_reduce_fusion), channel_id=1, replica_groups=mesh['region_0'=4,'region_1'=8,'tm_0'=8,'tm_1'=2] {'region_0'}, use_global_device_ids=true, to_apply=%region_16.18 | all-reduce | flops 1 | bytes 8 | tf_op jit(solution)/shard_map/psum | solution.py:34
  293.1 17.2 %psum.137 = f32[]{:T(128)} all-reduce(f32[]{:T(128)} %psum.136), channel_id=1, replica_groups=mesh['region_0'=4,'region_1'=8,'tm_0'=8,'tm_1'=2] {'region_1'}, use_global_device_ids=true, to_apply=%region_17.19 | all-reduce | flops 1 | bytes 8 | tf_op jit(solution)/shard_map/psum | solution.py:34
  310.3 11.6 %psum.138 = f32[]{:T(128)} all-reduce(f32[]{:T(128)} %psum.137), channel_id=1, replica_groups=mesh['region_0'=4,'region_1'=8,'tm_0'=8,'tm_1'=2] {'tm_0'}, use_global_device_ids=true, to_apply=%region_18.20 | all-reduce | flops 1 | bytes 8 | tf_op jit(solution)/shard_map/psum | solution.py:34
  321.9 11.5 %psum.139 = f32[]{:T(128)} all-reduce(f32[]{:T(128)} %psum.138), channel_id=1, replica_groups=mesh['region_0'=4,'region_1'=8,'tm_0'=8,'tm_1'=2] {'tm_1'}, use_global_device_ids=true, to_apply=%region_19.21 | all-reduce | flops 1 | bytes 8 | tf_op jit(solution)/shard_map/psum | solution.py:34
  (73 shorter events, 33.6 us)
Async XLA Ops:
  7.2 53.3 %all-gather.3.cloned.1.call-start = ((), (), s32[]{:S(2)}) async-start(), calls=%async_computation.6 | async-start | bytes 5013504 | tf_op jit(solution)/shard_map/all_gather | solution.py:53
  7.9 94.4 %all-gather.5.cloned.1.call-start = ((), (), s32[]{:S(2)}) async-start(), calls=%async_computation.7 | async-start | bytes 2359296 | tf_op jit(solution)/shard_map/all_gather | solution.py:28
  19.3 11.2 %collective-permute-start = (bf16[64,1024]{1,0:T(8,128)(2,1)S(1)}, bf16[64,1024]{1,0:T(8,128)(2,1)S(1)}, u32[]{:S(2)}, u32[]{:S(2)}) collective-permute-start(bf16[64,1024]{1,0:T(8,128)(2,1)S(1)} %get-tuple-element.26), channel_id=1, source_target_pairs={{0,16},{16,32},{32,48},{48,64},{64,80},{80,96},{96,112},{112,128},... | collective-permute-start | bytes 393224 | tf_op jit(solution)/shard_map/ppermute | solution.py:20
  21.2 10.2 %collective-permute-start.1 = (bf16[64,1024]{1,0:T(8,128)(2,1)S(1)}, bf16[64,1024]{1,0:T(8,128)(2,1)S(1)}, u32[]{:S(2)}, u32[]{:S(2)}) collective-permute-start(bf16[64,1024]{1,0:T(8,128)(2,1)S(1)} %get-tuple-element.27), channel_id=1, source_target_pairs={{16,0},{32,16},{48,32},{64,48},{80,64},{96,80},{112,96},{128,112},... | collective-permute-start | bytes 393224 | tf_op jit(solution)/shard_map/ppermute | solution.py:21
  65.5 36.9 %all-to-all-start = ((bf16[64,16,1,128]{3,0,2,1:T(8,128)(2,1)}), bf16[64,16,1,128]{3,0,2,1:T(8,128)(2,1)S(1)}, u32[]{:S(2)}, u32[]{:S(2)}) async-start(bf16[64,16,1,128]{3,0,2,1:T(8,128)(2,1)} %fusion.36), calls=%async_computation | async-start | bytes 524288 | tf_op jit(solution)/shard_map/all_to_all | solution.py:75
  106.2 20.8 %copy-start.3 = (f32[64,2048]{1,0:T(8,128)S(1)}, f32[64,2048]{1,0:T(8,128)}, u32[]{:S(2)}) copy-start(f32[64,2048]{1,0:T(8,128)} %param.8) | copy-start | bytes 1572868
  106.2 20.8 %copy-start.5 = (f32[64,2048]{1,0:T(8,128)S(1)}, f32[64,2048]{1,0:T(8,128)}, u32[]{:S(2)}) copy-start(f32[64,2048]{1,0:T(8,128)} %param.7) | copy-start | bytes 1572868
  127.3 11.4 %collective-permute-start.2 = (bf16[64,1024]{1,0:T(8,128)(2,1)S(1)}, bf16[64,1024]{1,0:T(8,128)(2,1)S(1)}, u32[]{:S(2)}, u32[]{:S(2)}) collective-permute-start(bf16[64,1024]{1,0:T(8,128)(2,1)S(1)} %get-tuple-element.24), channel_id=1, source_target_pairs={{0,16},{16,32},{32,48},{48,64},{64,80},{80,96},{96,112},{112,128},... | collective-permute-start | bytes 393224 | tf_op jit(solution)/shard_map/ppermute | solution.py:20
  130.6 9.5 %collective-permute-start.3 = (bf16[64,1024]{1,0:T(8,128)(2,1)S(1)}, bf16[64,1024]{1,0:T(8,128)(2,1)S(1)}, u32[]{:S(2)}, u32[]{:S(2)}) collective-permute-start(bf16[64,1024]{1,0:T(8,128)(2,1)S(1)} %get-tuple-element.25), channel_id=1, source_target_pairs={{16,0},{32,16},{48,32},{64,48},{80,64},{96,80},{112,96},{128,112},... | collective-permute-start | bytes 393224 | tf_op jit(solution)/shard_map/ppermute | solution.py:21
  142.7 19.8 %copy-start = (bf16[1024,1024]{1,0:T(8,128)(2,1)S(1)}, bf16[1024,1024]{1,0:T(8,128)(2,1)}, u32[]{:S(2)}) copy-start(bf16[1024,1024]{1,0:T(8,128)(2,1)} %all-gather.5.cloned.1.call-done) | copy-start | bytes 6291460
  179.4 62.0 %copy-start.1 = (f32[64,16,1,1,128]{4,1,0,3,2:T(8,128)}, f32[64,16,1,1,128]{4,1,0,3,2:T(8,128)S(1)}, u32[]{:S(2)}) copy-start(f32[64,16,1,1,128]{4,1,0,3,2:T(8,128)S(1)} %copy.53) | copy-start | bytes 1572868
  231.4 9.9 %collective-permute-start.4 = (bf16[64,1024]{1,0:T(8,128)(2,1)S(1)}, bf16[64,1024]{1,0:T(8,128)(2,1)S(1)}, u32[]{:S(2)}, u32[]{:S(2)}) collective-permute-start(bf16[64,1024]{1,0:T(8,128)(2,1)S(1)} %get-tuple-element.22), channel_id=1, source_target_pairs={{0,16},{16,32},{32,48},{48,64},{64,80},{80,96},{96,112},{112,128},... | collective-permute-start | bytes 393224 | tf_op jit(solution)/shard_map/ppermute | solution.py:20
  233.3 8.9 %collective-permute-start.5 = (bf16[64,1024]{1,0:T(8,128)(2,1)S(1)}, bf16[64,1024]{1,0:T(8,128)(2,1)S(1)}, u32[]{:S(2)}, u32[]{:S(2)}) collective-permute-start(bf16[64,1024]{1,0:T(8,128)(2,1)S(1)} %get-tuple-element.23), channel_id=1, source_target_pairs={{16,0},{32,16},{48,32},{64,48},{80,64},{96,80},{112,96},{128,112},... | collective-permute-start | bytes 393224 | tf_op jit(solution)/shard_map/ppermute | solution.py:21
  270.1 15.3 %copy-start.2 = (f32[64,16,1,1,128]{4,1,0,3,2:T(8,128)S(1)}, f32[64,16,1,1,128]{4,1,0,3,2:T(8,128)}, u32[]{:S(2)}) copy-start(f32[64,16,1,1,128]{4,1,0,3,2:T(8,128)} %copy-done.1) | copy-start | bytes 1572868
  284.6 49.4 %copy-start.4 = (f32[64,2048]{1,0:T(8,128)S(1)}, f32[64,2048]{1,0:T(8,128)}, u32[]{:S(2)}) copy-start(f32[64,2048]{1,0:T(8,128)} %param.8) | copy-start | bytes 1572868
Sparse Core Ops, SparseCore 0:
  10.1 50.3 all-gather.2
  62.5 39.7 all-gather.4
where the time goes:
time: 343 us; the launch traced here: 342 us
  blocking collectives  186 us (54%)
  waiting for transfers between devices  67.4 us (20%)
  starting transfers between devices  32.7 us (10%)
  matrix products  19.2 us (6%)
  between operations  18.8 us (5%)
  local copies, waits for them, and re-layouts  9.38 us (3%)
  other arithmetic  8.5 us (2%)
    psum x8, blocking collectives, one_axis_at_a_time(): value = lax.psum(value, axis)  94.3 us
    all_to_all x3, blocking collectives, operate(): lax.all_to_all(blended, TM, split_axis=0, concat_axis=1, tiled=True)  48.7 us
    all_to_all x2, blocking collectives, operate(): lax.all_to_all(spatial, TM, split_axis=1, concat_axis=0, tiled=True)  33.1 us
    all_gather x1, waiting for transfers between devices, gather_axes(): value = lax.all_gather(value, axis, axis=dim, tiled=True)  31.9 us
    all_gather x1, waiting for transfers between devices, local(): region_blocks = lax.all_gather(blocks, TM, axis=0, tiled=True)  27.8 us
    ppermute x3, starting transfers between devices, with_halo(): after = lax.ppermute(initial, axis, down)  20.6 us
    dot_general x3, matrix products, operate(): jnp.einsum('hrkb,rkab->hra', tile_stack, region_blocks, preferred_element...  15.1 us
    all_gather x1, blocking collectives, gather_axes(): value = lax.all_gather(value, axis, axis=dim, tiled=True)  10.2 us
  transfers between devices with their start and end apart: 9, of which 8 were waited for; matrix products, arithmetic and copies ran while one was open for 2% of the time, Pallas kernels for 0%

commit v1 on v0

--- a/solution.py
+++ b/solution.py
@@ -73,7 +73,10 @@
         )
         spatial = spatial.astype(jnp.bfloat16).reshape(hour_slice, tm_count, own_rows, tile_width)
         blended = temporal(lax.all_to_all(spatial, TM, split_axis=1, concat_axis=0, tiled=True))
-        returned = lax.all_to_all(blended, TM, split_axis=0, concat_axis=1, tiled=True)
+        returned = jnp.concatenate(
+            lax.all_to_all(jnp.stack(jnp.split(blended, lax.axis_size(TM), axis=0)), TM, 0, 0),
+            axis=1,
+        )
         return current + returned.reshape(hour_slice, site_count).astype(jnp.float32)
 
     solution = initial

time: 343 us -> 342 us (level)
  no operation moved by 1% of the time
where the time goes in v1:
time: 342 us; the launch traced here: 341 us
  blocking collectives  186 us (54%)
  waiting for transfers between devices  67.4 us (20%)
  starting transfers between devices  32.7 us (10%)
  matrix products  19.2 us (6%)
  between operations  19.1 us (6%)
  local copies, waits for them, and re-layouts  10.7 us (3%)
  other arithmetic  6.13 us (2%)
    psum x8, blocking collectives, one_axis_at_a_time(): value = lax.psum(value, axis)  94.3 us
    all_to_all x3, blocking collectives, operate(): lax.all_to_all(jnp.stack(jnp.split(blended, lax.axis_size(TM), axis=0)),...  48.5 us
    all_to_all x2, blocking collectives, operate(): lax.all_to_all(spatial, TM, split_axis=1, concat_axis=0, tiled=True)  33.1 us
    all_gather x1, waiting for transfers between devices, gather_axes(): value = lax.all_gather(value, axis, axis=dim, tiled=True)  31.9 us
    all_gather x1, waiting for transfers between devices, local(): region_blocks = lax.all_gather(blocks, TM, axis=0, tiled=True)  27.8 us
    ppermute x3, starting transfers between devices, with_halo(): after = lax.ppermute(initial, axis, down)  20.6 us
    dot_general x3, matrix products, operate(): jnp.einsum('hrkb,rkab->hra', tile_stack, region_blocks, preferred_element...  15.1 us
    all_gather x1, blocking collectives, gather_axes(): value = lax.all_gather(value, axis, axis=dim, tiled=True)  10.2 us
  transfers between devices with their start and end apart: 9, of which 8 were waited for; matrix products, arithmetic and copies ran while one was open for 2% of the time, Pallas kernels for 0%

profile of v1, /device:TPU:1, one launch (start us, length us, event | category | flops | bytes accessed | tf_op | source)
XLA Modules:
  0.0 341.4 jit_solution(2667462321026639514)
XLA Ops:
  7.9 10.2 %all_gather.10 = bf16[128,1024]{1,0:T(8,128)(2,1)} all-gather(bf16[64,1024]{1,0:T(8,128)(2,1)} %param.11), channel_id=1, replica_groups=mesh['region_0'=4,'region_1'=8,'tm_0'=8,'tm_1'=2] {'tm_1'}, dimensions={0}, use_global_device_ids=true | all-gather | bytes 393216 | tf_op jit(solution)/shard_map/all_gather | solution.py:28
  21.2 7.5 %collective-permute-start.1 = (bf16[64,1024]{1,0:T(8,128)(2,1)S(1)}, bf16[64,1024]{1,0:T(8,128)(2,1)S(1)}, u32[]{:S(2)}, u32[]{:S(2)}) collective-permute-start(bf16[64,1024]{1,0:T(8,128)(2,1)S(1)} %get-tuple-element.27), channel_id=1, source_target_pairs={{16,0},{32,16},{48,32},{64,48},{80,64},{96,80},{112,96},{128,112},... | collective-permute-start | bytes 393224 | tf_op jit(solution)/shard_map/ppermute | solution.py:21
  32.6 27.8 %all-gather.3.cloned.1.call-done = bf16[16,9,128,128]{3,2,1,0:T(8,128)(2,1)} async-done(((bf16[1,9,128,128]{3,2,1,0:T(8,128)(2,1)}), bf16[16,9,128,128]{3,2,1,0:T(8,128)(2,1)}) %all-gather.3.cloned.1.call-update) | async-done | bytes 4718608 | tf_op jit(solution)/shard_map/all_gather | solution.py:53
  60.5 5.0 %fusion.36 = bf16[64,16,1,128]{3,0,2,1:T(8,128)(2,1)} fusion(bf16[16,9,128,128]{3,2,1,0:T(8,128)(2,1)} %all-gather.3.cloned.1.call-done, bf16[16,9,64,128]{3,2,1,0:T(8,128)(2,1)S(1)} %bitcast.354, pred[16,9]{1,0:T(8,128)(4,1)S(1)} %copy.52), kind=kOutput, calls=%fused_computation.30 | convolution fusion | flops 303300608 | bytes 7340176 | tf_op jit(solution)/shard_map/hrkb,rkab->hra/dot_general | solution.py:71
  65.5 5.0 %all-to-all-start = ((bf16[64,16,1,128]{3,0,2,1:T(8,128)(2,1)}), bf16[64,16,1,128]{3,0,2,1:T(8,128)(2,1)S(1)}, u32[]{:S(2)}, u32[]{:S(2)}) async-start(bf16[64,16,1,128]{3,0,2,1:T(8,128)(2,1)} %fusion.36), calls=%async_computation | async-start | bytes 524288 | tf_op jit(solution)/shard_map/all_to_all | solution.py:75
  70.5 31.9 %all-gather.5.cloned.1.call-done = bf16[1024,1024]{1,0:T(8,128)(2,1)} async-done(((bf16[128,1024]{1,0:T(8,128)(2,1)}), bf16[1024,1024]{1,0:T(8,128)(2,1)}) %all-gather.5.cloned.1.call-update) | async-done | bytes 2097168 | tf_op jit(solution)/shard_map/all_gather | solution.py:28
  106.0 19.9 %all_to_all.60 = bf16[16,64,1,1,128]{4,1,3,2,0:T(8,128)(2,1)S(1)} all-to-all(bf16[16,64,1,1,128]{4,1,3,2,0:T(8,128)(2,1)S(1)} %copy.56), channel_id=1, replica_groups=mesh['region_0'=4,'region_1'=8,'tm_0'=8,'tm_1'=2] {'tm_0','tm_1'}, dimensions={0} | all-to-all | bytes 524288 | tf_op jit(solution)/shard_map/all_to_all | solution.py:77
  126.5 3.3 collective-permute-start.2
  129.8 6.4 %collective-permute-start.3 = (bf16[64,1024]{1,0:T(8,128)(2,1)S(1)}, bf16[64,1024]{1,0:T(8,128)(2,1)S(1)}, u32[]{:S(2)}, u32[]{:S(2)}) collective-permute-start(bf16[64,1024]{1,0:T(8,128)(2,1)S(1)} %get-tuple-element.25), channel_id=1, source_target_pairs={{16,0},{32,16},{48,32},{64,48},{80,64},{96,80},{112,96},{128,112},... | collective-permute-start | bytes 393224 | tf_op jit(solution)/shard_map/ppermute | solution.py:21
  142.0 5.1 %fusion.39 = bf16[64,16,1,128]{3,0,2,1:T(8,128)(2,1)S(1)} fusion(bf16[16,9,128,128]{3,2,1,0:T(8,128)(2,1)} %all-gather.3.cloned.1.call-done, bf16[16,9,64,128]{3,2,1,0:T(8,128)(2,1)} %bitcast.356, pred[16,9]{1,0:T(8,128)(4,1)S(1)} %copy.52), kind=kOutput, calls=%fused_computation.31 | convolution fusion | flops 303300608 | bytes 7340176 | tf_op jit(solution)/shard_map/hrkb,rkab->hra/dot_general | solution.py:71
  147.1 14.7 %all_to_all.61 = bf16[64,16,1,128]{3,0,2,1:T(8,128)(2,1)S(1)} all-to-all(bf16[64,16,1,128]{3,0,2,1:T(8,128)(2,1)S(1)} %fusion.39), channel_id=1, replica_groups=mesh['region_0'=4,'region_1'=8,'tm_0'=8,'tm_1'=2] {'tm_0','tm_1'}, dimensions={1} | all-to-all | bytes 524288 | tf_op jit(solution)/shard_map/all_to_all | solution.py:75
  163.8 14.2 %all_to_all.62 = bf16[16,64,1,1,128]{4,1,3,2,0:T(8,128)(2,1)S(1)} all-to-all(bf16[16,64,1,1,128]{4,1,3,2,0:T(8,128)(2,1)S(1)} %copy.62), channel_id=1, replica_groups=mesh['region_0'=4,'region_1'=8,'tm_0'=8,'tm_1'=2] {'tm_0','tm_1'}, dimensions={0} | all-to-all | bytes 524288 | tf_op jit(solution)/shard_map/all_to_all | solution.py:77
  179.3 7.2 %all-reduce.2 = (f32[]{:T(128)}, f32[]{:T(128)}, f32[]{:T(128)}) all-reduce(f32[]{:T(128)} %get-tuple-element.5, f32[]{:T(128)} %get-tuple-element.4, f32[]{:T(128)} %get-tuple-element.3), channel_id=1, replica_groups=mesh['region_0'=4,'region_1'=8,'tm_0'=8,'tm_1'=2] {'region_0'}, use_global_device_ids=true, to_apply=%region_1.3 | all-reduce | flops 3 | bytes 24 | tf_op jit(solution)/shard_map/psum | solution.py:34
  186.6 16.8 %all-reduce.1 = (f32[]{:T(128)}, f32[]{:T(128)}, f32[]{:T(128)}) all-reduce(f32[]{:T(128)} %get-tuple-element.12, f32[]{:T(128)} %get-tuple-element.13, f32[]{:T(128)} %get-tuple-element.14), channel_id=1, replica_groups=mesh['region_0'=4,'region_1'=8,'tm_0'=8,'tm_1'=2] {'region_1'}, use_global_device_ids=true, to_apply=%region_2.4 | all-reduce | flops 3 | bytes 24 | tf_op jit(solution)/shard_map/psum | solution.py:34
  203.4 11.7 %all-reduce = (f32[]{:T(128)}, f32[]{:T(128)}, f32[]{:T(128)}) all-reduce(f32[]{:T(128)} %get-tuple-element.9, f32[]{:T(128)} %get-tuple-element.10, f32[]{:T(128)} %get-tuple-element.11), channel_id=1, replica_groups=mesh['region_0'=4,'region_1'=8,'tm_0'=8,'tm_1'=2] {'tm_0'}, use_global_device_ids=true, to_apply=%region_3.5 | all-reduce | flops 3 | bytes 24 | tf_op jit(solution)/shard_map/psum | solution.py:34
  215.1 11.5 %all-reduce.3 = (f32[]{:T(128)}, f32[]{:T(128)}, f32[]{:T(128)}) all-reduce(f32[]{:T(128)} %get-tuple-element.6, f32[]{:T(128)} %get-tuple-element.7, f32[]{:T(128)} %get-tuple-element.8), channel_id=1, replica_groups=mesh['region_0'=4,'region_1'=8,'tm_0'=8,'tm_1'=2] {'tm_1'}, use_global_device_ids=true, to_apply=%region_4.6 | all-reduce | flops 3 | bytes 24 | tf_op jit(solution)/shard_map/psum | solution.py:34
  232.6 6.7 %collective-permute-start.5 = (bf16[64,1024]{1,0:T(8,128)(2,1)S(1)}, bf16[64,1024]{1,0:T(8,128)(2,1)S(1)}, u32[]{:S(2)}, u32[]{:S(2)}) collective-permute-start(bf16[64,1024]{1,0:T(8,128)(2,1)S(1)} %get-tuple-element.23), channel_id=1, source_target_pairs={{16,0},{32,16},{48,32},{64,48},{80,64},{96,80},{112,96},{128,112},... | collective-permute-start | bytes 393224 | tf_op jit(solution)/shard_map/ppermute | solution.py:21
  244.2 5.0 %fusion.42 = bf16[64,16,1,128]{3,0,2,1:T(8,128)(2,1)S(1)} fusion(bf16[16,9,128,128]{3,2,1,0:T(8,128)(2,1)} %all-gather.3.cloned.1.call-done, bf16[16,9,64,128]{3,2,1,0:T(8,128)(2,1)} %bitcast.355, pred[16,9]{1,0:T(8,128)(4,1)S(1)} %copy.52), kind=kOutput, calls=%fused_computation.32 | convolution fusion | flops 303300608 | bytes 7340176 | tf_op jit(solution)/shard_map/hrkb,rkab->hra/dot_general | solution.py:71
  249.2 18.4 %all_to_all.63 = bf16[64,16,1,128]{3,0,2,1:T(8,128)(2,1)S(1)} all-to-all(bf16[64,16,1,128]{3,0,2,1:T(8,128)(2,1)S(1)} %fusion.42), channel_id=1, replica_groups=mesh['region_0'=4,'region_1'=8,'tm_0'=8,'tm_1'=2] {'tm_0','tm_1'}, dimensions={1} | all-to-all | bytes 524288 | tf_op jit(solution)/shard_map/all_to_all | solution.py:75
  269.6 14.4 %all_to_all.64 = bf16[16,64,1,1,128]{4,1,3,2,0:T(8,128)(2,1)S(1)} all-to-all(bf16[16,64,1,1,128]{4,1,3,2,0:T(8,128)(2,1)S(1)} %copy.68), channel_id=1, replica_groups=mesh['region_0'=4,'region_1'=8,'tm_0'=8,'tm_1'=2] {'tm_0','tm_1'}, dimensions={0} | all-to-all | bytes 524288 | tf_op jit(solution)/shard_map/all_to_all | solution.py:77
  285.4 6.7 %psum.136 = f32[]{:T(128)} all-reduce(f32[]{:T(128)} %multiply_reduce_fusion), channel_id=1, replica_groups=mesh['region_0'=4,'region_1'=8,'tm_0'=8,'tm_1'=2] {'region_0'}, use_global_device_ids=true, to_apply=%region_16.18 | all-reduce | flops 1 | bytes 8 | tf_op jit(solution)/shard_map/psum | solution.py:34
  292.1 17.2 %psum.137 = f32[]{:T(128)} all-reduce(f32[]{:T(128)} %psum.136), channel_id=1, replica_groups=mesh['region_0'=4,'region_1'=8,'tm_0'=8,'tm_1'=2] {'region_1'}, use_global_device_ids=true, to_apply=%region_17.19 | all-reduce | flops 1 | bytes 8 | tf_op jit(solution)/shard_map/psum | solution.py:34
  309.3 11.6 %psum.138 = f32[]{:T(128)} all-reduce(f32[]{:T(128)} %psum.137), channel_id=1, replica_groups=mesh['region_0'=4,'region_1'=8,'tm_0'=8,'tm_1'=2] {'tm_0'}, use_global_device_ids=true, to_apply=%region_18.20 | all-reduce | flops 1 | bytes 8 | tf_op jit(solution)/shard_map/psum | solution.py:34
  320.9 11.5 %psum.139 = f32[]{:T(128)} all-reduce(f32[]{:T(128)} %psum.138), channel_id=1, replica_groups=mesh['region_0'=4,'region_1'=8,'tm_0'=8,'tm_1'=2] {'tm_1'}, use_global_device_ids=true, to_apply=%region_19.21 | all-reduce | flops 1 | bytes 8 | tf_op jit(solution)/shard_map/psum | solution.py:34
  (108 shorter events, 32.6 us)
Async XLA Ops:
  7.2 53.3 %all-gather.3.cloned.1.call-start = ((), (), s32[]{:S(2)}) async-start(), calls=%async_computation.6 | async-start | bytes 5013504 | tf_op jit(solution)/shard_map/all_gather | solution.py:53
  7.9 94.4 %all-gather.5.cloned.1.call-start = ((), (), s32[]{:S(2)}) async-start(), calls=%async_computation.7 | async-start | bytes 2359296 | tf_op jit(solution)/shard_map/all_gather | solution.py:28
  19.3 11.2 %collective-permute-start = (bf16[64,1024]{1,0:T(8,128)(2,1)S(1)}, bf16[64,1024]{1,0:T(8,128)(2,1)S(1)}, u32[]{:S(2)}, u32[]{:S(2)}) collective-permute-start(bf16[64,1024]{1,0:T(8,128)(2,1)S(1)} %get-tuple-element.26), channel_id=1, source_target_pairs={{0,16},{16,32},{32,48},{48,64},{64,80},{80,96},{96,112},{112,128},... | collective-permute-start | bytes 393224 | tf_op jit(solution)/shard_map/ppermute | solution.py:20
  21.2 10.2 %collective-permute-start.1 = (bf16[64,1024]{1,0:T(8,128)(2,1)S(1)}, bf16[64,1024]{1,0:T(8,128)(2,1)S(1)}, u32[]{:S(2)}, u32[]{:S(2)}) collective-permute-start(bf16[64,1024]{1,0:T(8,128)(2,1)S(1)} %get-tuple-element.27), channel_id=1, source_target_pairs={{16,0},{32,16},{48,32},{64,48},{80,64},{96,80},{112,96},{128,112},... | collective-permute-start | bytes 393224 | tf_op jit(solution)/shard_map/ppermute | solution.py:21
  65.5 36.9 %all-to-all-start = ((bf16[64,16,1,128]{3,0,2,1:T(8,128)(2,1)}), bf16[64,16,1,128]{3,0,2,1:T(8,128)(2,1)S(1)}, u32[]{:S(2)}, u32[]{:S(2)}) async-start(bf16[64,16,1,128]{3,0,2,1:T(8,128)(2,1)} %fusion.36), calls=%async_computation | async-start | bytes 524288 | tf_op jit(solution)/shard_map/all_to_all | solution.py:75
  104.7 21.5 %copy-start.3 = (f32[64,2048]{1,0:T(8,128)S(1)}, f32[64,2048]{1,0:T(8,128)}, u32[]{:S(2)}) copy-start(f32[64,2048]{1,0:T(8,128)} %param.8) | copy-start | bytes 1572868
  104.8 21.5 %copy-start.5 = (f32[64,2048]{1,0:T(8,128)S(1)}, f32[64,2048]{1,0:T(8,128)}, u32[]{:S(2)}) copy-start(f32[64,2048]{1,0:T(8,128)} %param.7) | copy-start | bytes 1572868
  126.5 11.4 %collective-permute-start.2 = (bf16[64,1024]{1,0:T(8,128)(2,1)S(1)}, bf16[64,1024]{1,0:T(8,128)(2,1)S(1)}, u32[]{:S(2)}, u32[]{:S(2)}) collective-permute-start(bf16[64,1024]{1,0:T(8,128)(2,1)S(1)} %get-tuple-element.24), channel_id=1, source_target_pairs={{0,16},{16,32},{32,48},{48,64},{64,80},{80,96},{96,112},{112,128},... | collective-permute-start | bytes 393224 | tf_op jit(solution)/shard_map/ppermute | solution.py:20
  129.8 9.5 %collective-permute-start.3 = (bf16[64,1024]{1,0:T(8,128)(2,1)S(1)}, bf16[64,1024]{1,0:T(8,128)(2,1)S(1)}, u32[]{:S(2)}, u32[]{:S(2)}) collective-permute-start(bf16[64,1024]{1,0:T(8,128)(2,1)S(1)} %get-tuple-element.25), channel_id=1, source_target_pairs={{16,0},{32,16},{48,32},{64,48},{80,64},{96,80},{112,96},{128,112},... | collective-permute-start | bytes 393224 | tf_op jit(solution)/shard_map/ppermute | solution.py:21
  142.0 19.8 %copy-start = (bf16[1024,1024]{1,0:T(8,128)(2,1)S(1)}, bf16[1024,1024]{1,0:T(8,128)(2,1)}, u32[]{:S(2)}) copy-start(bf16[1024,1024]{1,0:T(8,128)(2,1)} %all-gather.5.cloned.1.call-done) | copy-start | bytes 6291460
  178.4 62.2 %copy-start.1 = (f32[64,16,1,1,128]{4,1,0,3,2:T(8,128)}, f32[64,16,1,1,128]{4,1,0,3,2:T(8,128)S(1)}, u32[]{:S(2)}) copy-start(f32[64,16,1,1,128]{4,1,0,3,2:T(8,128)S(1)} %copy.63) | copy-start | bytes 1572868
  230.7 9.9 %collective-permute-start.4 = (bf16[64,1024]{1,0:T(8,128)(2,1)S(1)}, bf16[64,1024]{1,0:T(8,128)(2,1)S(1)}, u32[]{:S(2)}, u32[]{:S(2)}) collective-permute-start(bf16[64,1024]{1,0:T(8,128)(2,1)S(1)} %get-tuple-element.22), channel_id=1, source_target_pairs={{0,16},{16,32},{32,48},{48,64},{64,80},{80,96},{96,112},{112,128},... | collective-permute-start | bytes 393224 | tf_op jit(solution)/shard_map/ppermute | solution.py:20
  232.6 8.9 %collective-permute-start.5 = (bf16[64,1024]{1,0:T(8,128)(2,1)S(1)}, bf16[64,1024]{1,0:T(8,128)(2,1)S(1)}, u32[]{:S(2)}, u32[]{:S(2)}) collective-permute-start(bf16[64,1024]{1,0:T(8,128)(2,1)S(1)} %get-tuple-element.23), channel_id=1, source_target_pairs={{16,0},{32,16},{48,32},{64,48},{80,64},{96,80},{112,96},{128,112},... | collective-permute-start | bytes 393224 | tf_op jit(solution)/shard_map/ppermute | solution.py:21
  268.4 16.0 %copy-start.2 = (f32[64,16,1,1,128]{4,1,0,3,2:T(8,128)S(1)}, f32[64,16,1,1,128]{4,1,0,3,2:T(8,128)}, u32[]{:S(2)}) copy-start(f32[64,16,1,1,128]{4,1,0,3,2:T(8,128)} %copy-done.1) | copy-start | bytes 1572868
  269.4 63.7 %copy-start.4 = (f32[64,2048]{1,0:T(8,128)S(1)}, f32[64,2048]{1,0:T(8,128)}, u32[]{:S(2)}) copy-start(f32[64,2048]{1,0:T(8,128)} %param.8) | copy-start | bytes 1572868
Sparse Core Ops, SparseCore 0:
  10.1 50.3 all-gather.2
  62.5 39.7 all-gather.4
